TPU v7x, 32 devices: a whole 2x2x4 slice. The times are simulated.
32 devices in a mesh: groups: 2 (over y), dp: 4 (over x, core), expert: 4 (over z).
Axes of the slice: x: 2, y: 2, z: 4, core: 2. Of those that a mesh axis runs over, the one named last changes fastest.
Arguments:
- tokens: bfloat16 [256, 2048], P(('groups', 'dp', 'expert')), parts along dimension 0, may hold values from -3.5 to 3.5
- routes: int32 [256, 8], P('groups'), parts along dimension 0, may hold values from 0 to 15, all different within a row; in each aligned block of 8 rows (0 to 7, 8 to 15, ...) at most 8 rows name the same one
- gates: float32 [256, 8], P(('groups', 'dp', 'expert')), parts along dimension 0, may hold values from 0.1 to 1
- valid: int32 [256], P('groups'), parts along dimension 0, may hold values 0 or 1
- norm_gain: float32 [2048], replicated, may hold values from 0.5 to 1.5
- final_gain: float32 [2048], replicated, may hold values from 0.5 to 1.5
- w_gate: bfloat16 [16, 2048, 1024], P('expert', None, 'dp'), may hold values from -0.125 to 0.125
- w_up: bfloat16 [16, 2048, 1024], P('expert', None, 'dp'), may hold values from -0.125 to 0.125
- w_down: bfloat16 [16, 1024, 2048], P('expert', 'dp'), may hold values from -0.1875 to 0.1875
- head_weight: bfloat16 [2048, 10240], P(None, ('dp', 'expert')), as said below
- student_logits: bfloat16 [256, 10240], P('groups', ('dp', 'expert')), parts along dimension 0, may hold values from -24 to 220
Outputs:
- reverse_kl: float32 [256], P('groups'), parts along dimension 0
- logit_grad: bfloat16 [256, 10240], P('groups', ('dp', 'expert')), parts along dimension 0
There are 2 independent parts, one for each index of `groups`. A program takes and returns all parts, laid end to end along the dimension named above; an argument that names none is the same for every part. Nothing has to cross between parts.
Inputs may be any that keep to these rules, and one draw needn't show every extreme that they name: Each token names 8 different experts. In the 8 tokens of one device (aligned blocks of rows), no expert is named by more than 8 routes, a bound that some block reaches. `head_weight`: entries are of order one over the square root of 2048.
All inputs are finite; a program needn't handle non-finite values.
Results may differ from a plain program's by a relative error of at most 0.015.
Values may be sent and summed in bfloat16 or wider, within the bound.
No kernel may reach another device: no remote copies, remote signals or barrier semaphores. Data moves between devices by JAX's collectives and lax.ppermute only.
A program may use at most 64 MiB of HBM per device.

v0:
```python
import jax
import jax.numpy as jnp
from jax import lax
from jax.sharding import PartitionSpec as P

epsilon = 1e-06


def rms_scale(values, gain_vector):
    mean_square = jnp.mean(values * values, axis=-1, keepdims=True)
    return values * lax.rsqrt(mean_square + epsilon) * gain_vector


def slot_table(route_rows, expert_count, capacity):
    block_count, tok_count, route_count = route_rows.shape
    flat_routes = route_rows.reshape(block_count, tok_count * route_count)
    experts_iota = jnp.arange(expert_count, dtype=jnp.int32)
    onehot = (flat_routes[:, :, None] == experts_iota[None, None, :]).astype(jnp.int32)
    earlier = jnp.cumsum(onehot, axis=1) - onehot
    slot_rank = jnp.sum(earlier * onehot, axis=2)
    slot_index = flat_routes * capacity + slot_rank
    slots_iota = jnp.arange(expert_count * capacity, dtype=jnp.int32)
    slot_hot = (slot_index[:, :, None] == slots_iota[None, None, :]).astype(jnp.float32)
    return slot_hot.reshape(block_count, tok_count, route_count, expert_count * capacity)


def body(
    tokens,
    routes,
    gates,
    valid,
    norm_gain,
    final_gain,
    w_gate,
    w_up,
    w_down,
    head_weight,
    student_logits,
):
    token_count = tokens.shape[0]
    feature_count = tokens.shape[1]
    route_count = routes.shape[1]
    expert_ranks = lax.axis_size("expert")
    local_experts = w_gate.shape[0]
    expert_count = local_experts * expert_ranks
    capacity = max(2, 2 * token_count * route_count // expert_count)
    slot_total = expert_count * capacity
    hidden_in = tokens.astype(jnp.float32)
    normed = rms_scale(hidden_in, norm_gain).astype(jnp.bfloat16)
    position = lax.axis_index(("dp", "expert"))
    own_routes = lax.dynamic_slice_in_dim(routes, position * token_count, token_count, 0)
    own_hot = slot_table(own_routes[None], expert_count, capacity)[0]
    placed = jnp.einsum(
        "tks,td->sd", own_hot.astype(jnp.bfloat16), normed, preferred_element_type=jnp.float32
    ).astype(jnp.bfloat16)
    placed = placed.reshape(expert_ranks, local_experts, capacity, feature_count)
    received = lax.all_to_all(placed, "expert", split_axis=0, concat_axis=0, tiled=True)
    gathered = lax.all_gather(received, "dp", axis=0, tiled=True)
    gate_part = jnp.einsum("rlcd,ldf->rlcf", gathered, w_gate, preferred_element_type=jnp.float32)
    up_part = jnp.einsum("rlcd,ldf->rlcf", gathered, w_up, preferred_element_type=jnp.float32)
    activation = (jax.nn.silu(gate_part) * up_part).astype(jnp.bfloat16)
    partial_out = lax.psum_scatter(
        jnp.einsum("rlcf,lfd->rlcd", activation, w_down, preferred_element_type=jnp.float32).astype(
            jnp.bfloat16
        ),
        "dp",
        scatter_dimension=0,
        tiled=True,
    )
    returned = lax.all_to_all(partial_out, "expert", split_axis=0, concat_axis=0, tiled=True)
    returned = returned.reshape(slot_total, feature_count).astype(jnp.float32)
    weights = gates / jnp.sum(gates, axis=1, keepdims=True)
    combine_map = jnp.einsum("tk,tks->ts", weights, own_hot, precision=lax.Precision.HIGHEST)
    combined = jnp.dot(combine_map, returned, precision=lax.Precision.HIGHEST)
    mixed = hidden_in + combined
    final_normed = rms_scale(mixed, final_gain).astype(jnp.bfloat16)
    teacher = jnp.dot(
        lax.all_gather(final_normed, ("dp", "expert"), axis=0, tiled=True),
        head_weight,
        preferred_element_type=jnp.float32,
    )
    student = student_logits.astype(jnp.float32)
    teacher_top, student_top = lax.pmax(
        (jnp.max(teacher, axis=1), jnp.max(student, axis=1)), ("dp", "expert")
    )
    teacher_exp = jnp.exp(teacher - teacher_top[:, None])
    student_exp = jnp.exp(student - student_top[:, None])
    local_sums = (
        jnp.sum(teacher_exp, axis=1),
        jnp.sum(student_exp, axis=1),
        jnp.sum(student_exp * (student - teacher), axis=1),
    )
    teacher_total, student_total, cross_term = lax.psum(
        (local_sums[0], local_sums[1], local_sums[2]), ("dp", "expert")
    )
    log_teacher = (teacher_top + jnp.log(teacher_total))[:, None]
    log_student = (student_top + jnp.log(student_total))[:, None]
    divergence = (cross_term / student_total)[:, None] - log_student + log_teacher
    student_prob = jnp.exp(student - log_student)
    valid_rows = valid.astype(jnp.float32)[:, None]
    logit_grad = (
        valid_rows * student_prob * (student - log_student - (teacher - log_teacher) - divergence)
    ).astype(jnp.bfloat16)
    return ((valid_rows * divergence)[:, 0], logit_grad)


def solution(mesh):
    placed = (
        P(("groups", "dp", "expert"), None),
        P("groups", None),
        P(("groups", "dp", "expert"), None),
        P("groups"),
        P(),
        P(),
        P("expert", None, "dp"),
        P("expert", None, "dp"),
        P("expert", "dp", None),
        P(None, ("dp", "expert")),
        P("groups", ("dp", "expert")),
    )
    return jax.shard_map(
        body,
        mesh=mesh,
        in_specs=placed,
        out_specs=(P("groups"), P("groups", ("dp", "expert"))),
        check_vma=False,
    )
```

profile of v0, /device:TPU:0, one launch (start us, length us, event | category | flops | bytes accessed | tf_op | source)
XLA Modules:
  0.0 242.4 jit_solution(7114839426524506998)
XLA Ops:
  7.2 0.0 copy-start
  7.2 0.0 all-gather.2.cloned.1.call-start
  7.2 0.9 constant_dynamic-slice_fusion.1
  8.1 0.1 copy.31
  8.2 0.1 eq.46
  8.3 0.1 fusion.49
  8.4 0.1 reduce_window_sum.11
  8.5 0.2 select_reduce_fusion
  8.7 0.1 reduce_sum.76
  8.7 0.1 convert_reduce_fusion
  8.9 0.9 fusion.42
  9.8 1.1 convolution_convert_fusion
  10.9 20.6 %all_to_all.10 = bf16[4,4,8,2048]{3,2,1,0:T(8,128)(2,1)S(1)} all-to-all(bf16[4,4,8,2048]{3,2,1,0:T(8,128)(2,1)S(1)} %bitcast.64), channel_id=1, replica_groups=mesh['groups'=2,'dp'=4,'expert'=4] {'expert'}, dimensions={0} | all-to-all | bytes 1048576 | tf_op jit(solution)/shard_map/all_to_all | solution.py:57
  31.5 0.8 copy.22
  32.3 0.0 all-gather.2.cloned.1.call-update
  32.4 0.0 all-reduce.5.cloned.1.call-start
  32.4 21.8 %all-gather.2.cloned.1.call-done = bf16[16,4,8,2048]{3,2,0,1:T(8,128)(2,1)} async-done(((bf16[4,4,8,2048]{3,2,0,1:T(8,128)(2,1)}), bf16[16,4,8,2048]{3,2,0,1:T(8,128)(2,1)}) %all-gather.2.cloned.1.call-update) | async-done | bytes 2097168 | tf_op jit(solution)/shard_map/all_gather | solution.py:58
  54.2 3.5 %fusion.12 = f32[16,4,8,256]{3,2,0,1:T(8,128)S(1)} fusion(bf16[16,4,8,2048]{3,2,0,1:T(8,128)(2,1)} %all-gather.2.cloned.1.call-done, bf16[4,2048,256]{2,1,0:T(8,128)(2,1)} %param.17), kind=kOutput, calls=%fused_computation.10 | convolution fusion | flops 536870912 | bytes 6815744 | tf_op jit(solution)/shard_map/rlcd,ldf->rlcf/dot_general | solution.py:59
  57.7 0.0 copy-start.6
  57.7 6.7 %fusion.9 = bf16[16,4,8,2048]{3,2,0,1:T(8,128)(2,1)} fusion(bf16[4,256,2048]{2,1,0:T(8,128)(2,1)} %param.19, bf16[16,4,8,2048]{3,2,0,1:T(8,128)(2,1)} %all-gather.2.cloned.1.call-done, bf16[4,2048,256]{2,1,0:T(8,128)(2,1)} %param.18, f32[16,4,8,256]{3,2,0,1:T(8,128)S(1)} %fusion.12), kind=kOutput, calls=%fused_computation.7 | convolution fusion | flops 1075576832 | bytes 13107200 | tf_op jit(solution)/shard_map/rlcf,lfd->rlcd/dot_general | solution.py:63
  64.4 0.0 copy-start.5
  64.4 0.0 copy-start.3
  64.4 0.0 copy-start.1
  64.4 0.0 copy-start.2
  64.4 0.0 copy-start.4
  64.4 0.0 all-reduce.5.cloned.1.call-update
  64.5 0.0 copy-done.6
  64.5 0.6 dynamic-slice
  65.7 50.3 %all-reduce.5.cloned.1.call-done = bf16[16,4,8,2048]{3,2,0,1:T(8,128)(2,1)} async-done(((bf16[16,4,8,2048]{3,2,0,1:T(8,128)(2,1)}), bf16[16,4,8,2048]{3,2,0,1:T(8,128)(2,1)}) %all-reduce.5.cloned.1.call-update) | async-done | bytes 2097168
  116.0 1.1 constant_dynamic-slice_fusion
  117.1 0.8 copy.23
  117.9 4.6 %all-to-all-start.1 = ((bf16[4,4,8,2048]{3,2,1,0:T(8,128)(2,1)}), bf16[4,4,8,2048]{3,2,1,0:T(8,128)(2,1)S(1)}, u32[]{:S(2)}, u32[]{:S(2)}) async-start(bf16[4,4,8,2048]{3,2,1,0:T(8,128)(2,1)} %copy.23), calls=%async_computation.1 | async-start | bytes 1048576 | tf_op jit(solution)/shard_map/all_to_all | solution.py:70
  122.5 0.0 copy-done.5
  122.5 0.0 copy-done.3
  122.5 0.1 reduce_sum.74
  122.6 0.0 copy-done.1
  122.6 0.1 reduce_max.23
  122.7 0.1 broadcast_divide_fusion
  122.8 0.2 fusion.48
  123.0 13.7 %all-to-all-done.1 = bf16[4,4,8,2048]{3,2,1,0:T(8,128)(2,1)S(1)} async-done(((bf16[4,4,8,2048]{3,2,1,0:T(8,128)(2,1)}), bf16[4,4,8,2048]{3,2,1,0:T(8,128)(2,1)S(1)}, u32[]{:S(2)}, u32[]{:S(2)}) %all-to-all-start.1) | async-done | bytes 524320 | tf_op jit(solution)/shard_map/all_to_all | solution.py:70
  136.7 0.0 copy-done.2
  136.7 0.4 multiply_reduce_fusion
  137.2 0.0 copy-done.4
  137.2 0.1 multiply_convert_fusion
  137.3 33.7 %all_gather.7 = bf16[128,2048]{1,0:T(8,128)(2,1)S(1)} all-gather(bf16[8,2048]{1,0:T(8,128)(2,1)S(1)} %multiply_convert_fusion), channel_id=1, replica_groups=mesh['groups'=2,'dp'=4,'expert'=4] {'dp','expert'}, dimensions={0}, use_global_device_ids=true | all-gather | bytes 557056 | tf_op jit(solution)/shard_map/all_gather | solution.py:78
  171.0 0.0 copy-done
  171.0 0.7 fusion.52
  171.6 31.3 %all-reduce.2 = (f32[128]{0:T(128)S(1)}, f32[128]{0:T(128)S(1)}) all-reduce(f32[128]{0:T(128)S(1)} %get-tuple-element.16, bf16[128]{0:T(256)(128)(2,1)S(1)} %reduce_max.23), channel_id=1, replica_groups=mesh['groups'=2,'dp'=4,'expert'=4] {'dp','expert'}, use_global_device_ids=true, to_apply=%region_14.15 | all-reduce | flops 256 | bytes 1792 | tf_op jit(solution)/shard_map/pmax | solution.py:83
  202.9 0.3 fusion.40
  203.2 31.0 %all-reduce.1 = (f32[128]{0:T(128)S(1)}, f32[128]{0:T(128)S(1)}, f32[128]{0:T(128)S(1)}) all-reduce(f32[128]{0:T(128)S(1)} %get-tuple-element.3, f32[128]{0:T(128)S(1)} %get-tuple-element.4, f32[128]{0:T(128)S(1)} %get-tuple-element.2), channel_id=1, replica_groups=mesh['groups'=2,'dp'=4,'expert'=4] {'dp','expert'}, use_global_device_ids=true, to_apply=%region_16.17 | all-reduce | flops 384 | bytes 3072 | tf_op jit(solution)/shard_map/psum | solution.py:93
  234.2 0.5 convert_multiply_fusion.2
  234.7 0.8 fusion.35
  (4 shorter events, 0.0 us)
Async XLA Ops:
  7.2 163.8 %copy-start = (bf16[2048,640]{1,0:T(8,128)(2,1)S(1)}, bf16[2048,640]{1,0:T(8,128)(2,1)}, u32[]{:S(2)}) copy-start(bf16[2048,640]{1,0:T(8,128)(2,1)} %param.20) | copy-start | bytes 7864324
  7.2 47.0 %all-gather.2.cloned.1.call-start = ((), (), s32[]{:S(2)}) async-start(), calls=%async_computation.2 | async-start | bytes 2621440 | tf_op jit(solution)/shard_map/all_gather | solution.py:58
  32.4 83.6 %all-reduce.5.cloned.1.call-start = ((), (), s32[]{:S(2)}) async-start(), calls=%async_computation.3 | async-start | bytes 4194304
  57.7 6.7 %copy-start.6 = (u32[32]{0:T(128)S(1)}, u32[32]{0:T(128)}, u32[]{:S(2)}) copy-start(u32[32]{0:T(128)} %constant.39) | copy-start | bytes 388
  64.4 58.1 %copy-start.5 = (s32[128]{0:T(128)S(1)}, s32[128]{0:T(128)}, u32[]{:S(2)}) copy-start(s32[128]{0:T(128)} %param.14) | copy-start | bytes 1540
  64.4 58.1 %copy-start.3 = (f32[8,8]{1,0:T(8,128)S(1)}, f32[8,8]{1,0:T(8,128)}, u32[]{:S(2)}) copy-start(f32[8,8]{1,0:T(8,128)} %param.13) | copy-start | bytes 772
  64.4 58.2 %copy-start.1 = (bf16[128,640]{1,0:T(8,128)(2,1)S(1)}, bf16[128,640]{1,0:T(8,128)(2,1)}, u32[]{:S(2)}) copy-start(bf16[128,640]{1,0:T(8,128)(2,1)} %param.21) | copy-start | bytes 491524
  64.4 72.3 %copy-start.2 = (bf16[8,2048]{1,0:T(8,128)(2,1)S(1)}, bf16[8,2048]{1,0:T(8,128)(2,1)}, u32[]{:S(2)}) copy-start(bf16[8,2048]{1,0:T(8,128)(2,1)} %param.11) | copy-start | bytes 98308
  64.4 72.8 %copy-start.4 = (f32[2048]{0:T(1024)S(1)}, f32[2048]{0:T(1024)}, u32[]{:S(2)}) copy-start(f32[2048]{0:T(1024)} %param.16) | copy-start | bytes 24580
  117.9 18.9 %all-to-all-start.1 = ((bf16[4,4,8,2048]{3,2,1,0:T(8,128)(2,1)}), bf16[4,4,8,2048]{3,2,1,0:T(8,128)(2,1)S(1)}, u32[]{:S(2)}, u32[]{:S(2)}) async-start(bf16[4,4,8,2048]{3,2,1,0:T(8,128)(2,1)} %copy.23), calls=%async_computation.1 | async-start | bytes 1048576 | tf_op jit(solution)/shard_map/all_to_all | solution.py:70
Sparse Core Ops, SparseCore 0:
  32.5 21.6 all-gather.1
  64.6 51.3 all-reduce.4
where the time goes:
time: 243 us; the launch traced here: 242 us
  blocking collectives  117 us (48%)
  waiting for transfers between devices  85.8 us (35%)
  between operations  14.8 us (6%)
  matrix products  12.6 us (5%)
  starting transfers between devices  4.68 us (2%)
  local copies, waits for them, and re-layouts  4.5 us (2%)
  other arithmetic  3.42 us (1%)
    unnamed x3, waiting for transfers between devices  50.3 us
    all_gather x1, blocking collectives, body(): lax.all_gather(final_normed, ('dp', 'expert'), axis=0, tiled=True)  33.7 us
    pmax x1, blocking collectives, body(): lax.pmax((jnp.max(teacher, axis=1), jnp.max(student, axis=1)), ('dp', 'ex...  31.3 us
    psum x1, blocking collectives, body(): lax.psum((local_sums[0], local_sums[1], local_sums[2]), ('dp', 'expert'))  31 us
    all_gather x1, waiting for transfers between devices, body(): gathered = lax.all_gather(received, 'dp', axis=0, tiled=True)  21.8 us
    all_to_all x1, blocking collectives, body(): lax.all_to_all(placed, 'expert', split_axis=0, concat_axis=0, tiled=True)  20.6 us
    all_to_all x1, waiting for transfers between devices, body(): lax.all_to_all(partial_out, 'expert', split_axis=0, concat_axis=0, tiled=...  13.7 us
    dot_general x1, matrix products, body(): jnp.einsum('rlcf,lfd->rlcd', activation, w_down, preferred_element_type=j...  6.65 us
  transfers between devices with their start and end apart: 3, of which 3 were waited for; matrix products, arithmetic and copies ran while one was open for 0% of the time, Pallas kernels for 0%

commit v1 on v0

--- a/solution.py
+++ b/solution.py
@@ -91,7 +91,7 @@
         jnp.sum(student_exp * (student - teacher), axis=1),
     )
     teacher_total, student_total, cross_term = lax.psum(
-        (local_sums[0], local_sums[1], local_sums[2]), ("dp", "expert")
+        lax.psum((local_sums[0], local_sums[1], local_sums[2]), "expert"), "dp"
     )
     log_teacher = (teacher_top + jnp.log(teacher_total))[:, None]
     log_student = (student_top + jnp.log(student_total))[:, None]

time: 243 us -> 227 us (0.934)
  blocking collectives: 117 us -> 101 us
    psum x1 -> x2, blocking collectives: 31 us -> 15.3 us  [the longest x1 9.63 us: body(): lax.psum((local_sums[0], local_sums[1], local_sums[2]), 'expert')]
where the time goes in v1:
time: 227 us
  blocking collectives  101 us (44%)
  waiting for transfers between devices  85.8 us (38%)
  between operations  14.8 us (7%)
  matrix products  12.6 us (6%)
  starting transfers between devices  4.68 us (2%)
  local copies, waits for them, and re-layouts  4.5 us (2%)
  other arithmetic  3.42 us (2%)
    unnamed x3, waiting for transfers between devices  50.3 us
    all_gather x1, blocking collectives, body(): lax.all_gather(final_normed, ('dp', 'expert'), axis=0, tiled=True)  33.7 us
    pmax x1, blocking collectives, body(): lax.pmax((jnp.max(teacher, axis=1), jnp.max(student, axis=1)), ('dp', 'ex...  31.3 us
    all_gather x1, waiting for transfers between devices, body(): gathered = lax.all_gather(received, 'dp', axis=0, tiled=True)  21.8 us
    all_to_all x1, blocking collectives, body(): lax.all_to_all(placed, 'expert', split_axis=0, concat_axis=0, tiled=True)  20.6 us
    all_to_all x1, waiting for transfers between devices, body(): lax.all_to_all(partial_out, 'expert', split_axis=0, concat_axis=0, tiled=...  13.7 us
    psum x1, blocking collectives, body(): lax.psum((local_sums[0], local_sums[1], local_sums[2]), 'expert')  9.63 us
    dot_general x1, matrix products, body(): jnp.einsum('rlcf,lfd->rlcd', activation, w_down, preferred_element_type=j...  6.65 us
  transfers between devices with their start and end apart: 3, of which 3 were waited for; matrix products, arithmetic and copies ran while one was open for 0% of the time, Pallas kernels for 0%

profile of v1, /device:TPU:0, one launch (start us, length us, event | category | flops | bytes accessed | tf_op | source)
XLA Modules:
  0.0 226.7 jit_solution(10388052228719843189)
XLA Ops:
  7.2 0.0 copy-start
  7.2 0.0 all-gather.2.cloned.1.call-start
  7.2 0.9 constant_dynamic-slice_fusion.1
  8.1 0.1 copy.31
  8.2 0.1 eq.46
  8.3 0.1 fusion.49
  8.4 0.1 reduce_window_sum.11
  8.5 0.2 select_reduce_fusion
  8.7 0.1 reduce_sum.76
  8.7 0.1 convert_reduce_fusion
  8.9 0.9 fusion.42
  9.8 1.1 convolution_convert_fusion
  10.9 20.6 %all_to_all.10 = bf16[4,4,8,2048]{3,2,1,0:T(8,128)(2,1)S(1)} all-to-all(bf16[4,4,8,2048]{3,2,1,0:T(8,128)(2,1)S(1)} %bitcast.64), channel_id=1, replica_groups=mesh['groups'=2,'dp'=4,'expert'=4] {'expert'}, dimensions={0} | all-to-all | bytes 1048576 | tf_op jit(solution)/shard_map/all_to_all | solution.py:57
  31.5 0.8 copy.22
  32.3 0.0 all-gather.2.cloned.1.call-update
  32.4 0.0 all-reduce.6.cloned.1.call-start
  32.4 21.8 %all-gather.2.cloned.1.call-done = bf16[16,4,8,2048]{3,2,0,1:T(8,128)(2,1)} async-done(((bf16[4,4,8,2048]{3,2,0,1:T(8,128)(2,1)}), bf16[16,4,8,2048]{3,2,0,1:T(8,128)(2,1)}) %all-gather.2.cloned.1.call-update) | async-done | bytes 2097168 | tf_op jit(solution)/shard_map/all_gather | solution.py:58
  54.2 3.5 %fusion.12 = f32[16,4,8,256]{3,2,0,1:T(8,128)S(1)} fusion(bf16[16,4,8,2048]{3,2,0,1:T(8,128)(2,1)} %all-gather.2.cloned.1.call-done, bf16[4,2048,256]{2,1,0:T(8,128)(2,1)} %param.17), kind=kOutput, calls=%fused_computation.10 | convolution fusion | flops 536870912 | bytes 6815744 | tf_op jit(solution)/shard_map/rlcd,ldf->rlcf/dot_general | solution.py:59
  57.7 0.0 copy-start.6
  57.7 6.7 %fusion.9 = bf16[16,4,8,2048]{3,2,0,1:T(8,128)(2,1)} fusion(bf16[4,256,2048]{2,1,0:T(8,128)(2,1)} %param.19, bf16[16,4,8,2048]{3,2,0,1:T(8,128)(2,1)} %all-gather.2.cloned.1.call-done, bf16[4,2048,256]{2,1,0:T(8,128)(2,1)} %param.18, f32[16,4,8,256]{3,2,0,1:T(8,128)S(1)} %fusion.12), kind=kOutput, calls=%fused_computation.7 | convolution fusion | flops 1075576832 | bytes 13107200 | tf_op jit(solution)/shard_map/rlcf,lfd->rlcd/dot_general | solution.py:63
  64.4 0.0 copy-start.5
  64.4 0.0 copy-start.3
  64.4 0.0 copy-start.1
  64.4 0.0 copy-start.2
  64.4 0.0 copy-start.4
  64.4 0.0 all-reduce.6.cloned.1.call-update
  64.5 0.0 copy-done.6
  64.5 0.6 dynamic-slice
  65.7 50.3 %all-reduce.6.cloned.1.call-done = bf16[16,4,8,2048]{3,2,0,1:T(8,128)(2,1)} async-done(((bf16[16,4,8,2048]{3,2,0,1:T(8,128)(2,1)}), bf16[16,4,8,2048]{3,2,0,1:T(8,128)(2,1)}) %all-reduce.6.cloned.1.call-update) | async-done | bytes 2097168
  116.0 1.1 constant_dynamic-slice_fusion
  117.1 0.8 copy.23
  117.9 4.6 %all-to-all-start.1 = ((bf16[4,4,8,2048]{3,2,1,0:T(8,128)(2,1)}), bf16[4,4,8,2048]{3,2,1,0:T(8,128)(2,1)S(1)}, u32[]{:S(2)}, u32[]{:S(2)}) async-start(bf16[4,4,8,2048]{3,2,1,0:T(8,128)(2,1)} %copy.23), calls=%async_computation.1 | async-start | bytes 1048576 | tf_op jit(solution)/shard_map/all_to_all | solution.py:70
  122.5 0.0 copy-done.5
  122.5 0.0 copy-done.3
  122.5 0.1 reduce_sum.74
  122.6 0.0 copy-done.1
  122.6 0.1 reduce_max.23
  122.7 0.1 broadcast_divide_fusion
  122.8 0.2 fusion.48
  123.0 13.7 %all-to-all-done.1 = bf16[4,4,8,2048]{3,2,1,0:T(8,128)(2,1)S(1)} async-done(((bf16[4,4,8,2048]{3,2,1,0:T(8,128)(2,1)}), bf16[4,4,8,2048]{3,2,1,0:T(8,128)(2,1)S(1)}, u32[]{:S(2)}, u32[]{:S(2)}) %all-to-all-start.1) | async-done | bytes 524320 | tf_op jit(solution)/shard_map/all_to_all | solution.py:70
  136.7 0.0 copy-done.2
  136.7 0.4 multiply_reduce_fusion
  137.2 0.0 copy-done.4
  137.2 0.1 multiply_convert_fusion
  137.3 33.7 %all_gather.7 = bf16[128,2048]{1,0:T(8,128)(2,1)S(1)} all-gather(bf16[8,2048]{1,0:T(8,128)(2,1)S(1)} %multiply_convert_fusion), channel_id=1, replica_groups=mesh['groups'=2,'dp'=4,'expert'=4] {'dp','expert'}, dimensions={0}, use_global_device_ids=true | all-gather | bytes 557056 | tf_op jit(solution)/shard_map/all_gather | solution.py:78
  171.0 0.0 copy-done
  171.0 0.7 fusion.52
  171.6 31.3 %all-reduce.1 = (f32[128]{0:T(128)S(1)}, f32[128]{0:T(128)S(1)}) all-reduce(f32[128]{0:T(128)S(1)} %get-tuple-element.19, bf16[128]{0:T(256)(128)(2,1)S(1)} %reduce_max.23), channel_id=1, replica_groups=mesh['groups'=2,'dp'=4,'expert'=4] {'dp','expert'}, use_global_device_ids=true, to_apply=%region_16.17 | all-reduce | flops 256 | bytes 1792 | tf_op jit(solution)/shard_map/pmax | solution.py:83
  202.9 0.3 fusion.40
  203.2 9.6 %all-reduce.2 = (f32[128]{0:T(128)S(1)}, f32[128]{0:T(128)S(1)}, f32[128]{0:T(128)S(1)}) all-reduce(f32[128]{0:T(128)S(1)} %get-tuple-element.3, f32[128]{0:T(128)S(1)} %get-tuple-element.4, f32[128]{0:T(128)S(1)} %get-tuple-element.2), channel_id=1, replica_groups=mesh['groups'=2,'dp'=4,'expert'=4] {'expert'}, use_global_device_ids=true, to_apply=%region_18.19 | all-reduce | flops 384 | bytes 3072 | tf_op jit(solution)/shard_map/psum | solution.py:94
  212.9 5.7 %all-reduce.3 = (f32[128]{0:T(128)S(1)}, f32[128]{0:T(128)S(1)}, f32[128]{0:T(128)S(1)}) all-reduce(f32[128]{0:T(128)S(1)} %get-tuple-element.7, f32[128]{0:T(128)S(1)} %get-tuple-element.8, f32[128]{0:T(128)S(1)} %get-tuple-element.9), channel_id=1, replica_groups=mesh['groups'=2,'dp'=4,'expert'=4] {'dp'}, use_global_device_ids=true, to_apply=%region_19.20 | all-reduce | flops 384 | bytes 3072 | tf_op jit(solution)/shard_map/psum | solution.py:93
  218.5 0.5 convert_multiply_fusion.2
  219.0 0.8 fusion.35
  (4 shorter events, 0.0 us)
Async XLA Ops:
  7.2 163.8 %copy-start = (bf16[2048,640]{1,0:T(8,128)(2,1)S(1)}, bf16[2048,640]{1,0:T(8,128)(2,1)}, u32[]{:S(2)}) copy-start(bf16[2048,640]{1,0:T(8,128)(2,1)} %param.20) | copy-start | bytes 7864324
  7.2 47.0 %all-gather.2.cloned.1.call-start = ((), (), s32[]{:S(2)}) async-start(), calls=%async_computation.2 | async-start | bytes 2621440 | tf_op jit(solution)/shard_map/all_gather | solution.py:58
  32.4 83.6 %all-reduce.6.cloned.1.call-start = ((), (), s32[]{:S(2)}) async-start(), calls=%async_computation.3 | async-start | bytes 4194304
  57.7 6.7 %copy-start.6 = (u32[32]{0:T(128)S(1)}, u32[32]{0:T(128)}, u32[]{:S(2)}) copy-start(u32[32]{0:T(128)} %constant.39) | copy-start | bytes 388
  64.4 58.1 %copy-start.5 = (s32[128]{0:T(128)S(1)}, s32[128]{0:T(128)}, u32[]{:S(2)}) copy-start(s32[128]{0:T(128)} %param.14) | copy-start | bytes 1540
  64.4 58.1 %copy-start.3 = (f32[8,8]{1,0:T(8,128)S(1)}, f32[8,8]{1,0:T(8,128)}, u32[]{:S(2)}) copy-start(f32[8,8]{1,0:T(8,128)} %param.13) | copy-start | bytes 772
  64.4 58.2 %copy-start.1 = (bf16[128,640]{1,0:T(8,128)(2,1)S(1)}, bf16[128,640]{1,0:T(8,128)(2,1)}, u32[]{:S(2)}) copy-start(bf16[128,640]{1,0:T(8,128)(2,1)} %param.21) | copy-start | bytes 491524
  64.4 72.3 %copy-start.2 = (bf16[8,2048]{1,0:T(8,128)(2,1)S(1)}, bf16[8,2048]{1,0:T(8,128)(2,1)}, u32[]{:S(2)}) copy-start(bf16[8,2048]{1,0:T(8,128)(2,1)} %param.11) | copy-start | bytes 98308
  64.4 72.8 %copy-start.4 = (f32[2048]{0:T(1024)S(1)}, f32[2048]{0:T(1024)}, u32[]{:S(2)}) copy-start(f32[2048]{0:T(1024)} %param.16) | copy-start | bytes 24580
  117.9 18.9 %all-to-all-start.1 = ((bf16[4,4,8,2048]{3,2,1,0:T(8,128)(2,1)}), bf16[4,4,8,2048]{3,2,1,0:T(8,128)(2,1)S(1)}, u32[]{:S(2)}, u32[]{:S(2)}) async-start(bf16[4,4,8,2048]{3,2,1,0:T(8,128)(2,1)} %copy.23), calls=%async_computation.1 | async-start | bytes 1048576 | tf_op jit(solution)/shard_map/all_to_all | solution.py:70
Sparse Core Ops, SparseCore 0:
  32.5 21.6 all-gather.1
  64.6 51.3 all-reduce.5
